TPU v7x, 512 devices: a whole 4x4x16 slice. The times are simulated.
512 devices in a mesh: grp: 64 (over z, x_lo, core), rep: 8 (over y, x_hi).
Axes of the slice: x: 4 (x_hi: 2, x_lo: 2; x = x_hi * 2 + x_lo), y: 4, z: 16, core: 2. Of those that a mesh axis runs over, the one named last changes fastest.
Arguments:
- adjoint: bfloat16 [1024, 512], P('grp'), may hold values from -6 to 6
- active: int32 [1024, 512], P('grp'), may hold values 0 or 1
- counts: int32 [1024, 65536], P('rep', 'grp'), may hold values from 0 to 3, as said below
- src_degree: int32 [1024], P('rep'), may hold values from 8 to 256
- dst_degree: int32 [65536], P('grp'), may hold values from 8 to 256
- inputs: bfloat16 [65536, 512], P(('grp', 'rep')), may hold values from -6 to 6
- weight: bfloat16 [512, 512], replicated, may hold values from -0.25 to 0.25
Outputs:
- grad_input: bfloat16 [65536, 512], P(('grp', 'rep'))
- grad_weight: float32 [512, 512], P('rep')
Inputs may be any that keep to these rules, and one draw needn't show every extreme that they name: Edge counts; within an aligned tile of 16 source rows by 1024 destination columns the share of nonzero entries ranges from none to all, differing from tile to tile.
All inputs are finite; a program needn't handle non-finite values. No bound on the sum of `active` on one device may be relied on, other than what follows from the above.
Results may differ from a plain program's by a relative error of at most 0.0057.
Values may be sent and summed in bfloat16 or wider, within the bound.
A program may use at most 64 MiB of HBM per device.

v0:
```python
import jax
import jax.numpy as jnp
from jax import lax
from jax.sharding import PartitionSpec as P


def body(adjoint, active, counts, src_degree, dst_degree, inputs, weight):
    masked = (adjoint.astype(jnp.float32) * active.astype(jnp.float32)).astype(jnp.bfloat16)
    src_scale = lax.rsqrt(src_degree.astype(jnp.float32))
    dst_scale = lax.rsqrt(dst_degree.astype(jnp.float32))
    scaled = (counts.astype(jnp.float32) * src_scale[:, None] * dst_scale[None, :]).astype(
        jnp.bfloat16
    )
    my_scaled = lax.all_to_all(scaled, "rep", split_axis=1, concat_axis=0, tiled=True)
    all_masked = lax.all_gather(masked, "grp", axis=0, tiled=True)
    grad_pre = lax.dot_general(
        my_scaled, all_masked, (((0,), (0,)), ((), ())), preferred_element_type=jnp.float32
    )
    high = grad_pre.astype(jnp.bfloat16)
    low = (grad_pre - high.astype(jnp.float32)).astype(jnp.bfloat16)
    grad_input = lax.dot_general(
        high, weight, (((1,), (1,)), ((), ())), preferred_element_type=jnp.float32
    ).astype(jnp.bfloat16)
    vertex_total = inputs.shape[0] * lax.axis_size("grp") * lax.axis_size("rep")
    upper = lax.dot_general(
        inputs, high, (((0,), (0,)), ((), ())), preferred_element_type=jnp.float32
    )
    lower = lax.dot_general(
        inputs, low, (((0,), (0,)), ((), ())), preferred_element_type=jnp.float32
    )
    part = lax.psum_scatter(upper + lower, "rep", scatter_dimension=0, tiled=True)
    grad_weight = lax.psum(part, "grp")
    return (grad_input, grad_weight / vertex_total)


def solution(mesh):
    in_specs = (
        P("grp", None),
        P("grp", None),
        P("rep", "grp"),
        P("rep"),
        P("grp"),
        P(("grp", "rep"), None),
        P(),
    )
    out_specs = (P(("grp", "rep"), None), P("rep", None))
    return jax.shard_map(body, mesh=mesh, in_specs=in_specs, out_specs=out_specs, check_vma=False)
```

profile of v0, /device:TPU:1, one launch (start us, length us, event | category | flops | bytes accessed | tf_op | source)
XLA Modules:
  0.0 647.1 jit_solution(7749764605199366862)
XLA Ops:
  7.2 0.0 copy-start
  7.2 0.0 all-gather.2.cloned.1.call-start
  7.2 1.4 multiply_convert_fusion.1
  8.6 0.0 all-gather.2.cloned.1.call-update
  8.7 0.0 copy-start.3
  8.7 0.0 reduce-scatter.4.cloned.1.call-start
  8.7 1.2 copy.14
  10.0 0.2 multiply_convert_fusion
  10.2 15.2 %all_to_all.19 = bf16[128,8,128]{0,2,1:T(8,128)(2,1)S(1)} all-to-all(bf16[128,8,128]{0,2,1:T(8,128)(2,1)S(1)} %bitcast.13), channel_id=1, replica_groups=mesh['grp'=64,'rep'=8] {'rep'}, dimensions={1} | all-to-all | bytes 524288 | tf_op jit(solution)/shard_map/all_to_all | solution.py:14
  25.4 0.2 copy.15
  25.6 112.0 %all-gather.2.cloned.1.call-done = bf16[1024,512]{1,0:T(8,128)(2,1)} async-done(((bf16[16,512]{1,0:T(8,128)(2,1)}), bf16[1024,512]{1,0:T(8,128)(2,1)}) %all-gather.2.cloned.1.call-update) | async-done | bytes 1048592 | tf_op jit(solution)/shard_map/all_gather | solution.py:15
  137.6 1.6 fusion.5
  139.2 0.3 fusion.2
  139.5 0.3 fusion
  139.8 1.3 copy.17
  141.1 0.0 reduce-scatter.4.cloned.1.call-update
  141.2 0.0 all-reduce.2.cloned.1.call-start
  141.2 82.9 %reduce-scatter.4.cloned.1.call-done = f32[64,512]{1,0:T(8,128)} async-done(((f32[512,512]{1,0:T(8,128)}), f32[64,512]{1,0:T(8,128)}) %reduce-scatter.4.cloned.1.call-update) | async-done | bytes 131088
  224.1 1.7 copy.18
  225.8 0.0 all-reduce.2.cloned.1.call-update
  225.9 1.0 convolution_convert_fusion
  226.8 412.0 %all-reduce.2.cloned.1.call-done = f32[64,512]{0,1:T(8,128)} async-done(((f32[64,512]{0,1:T(8,128)}), f32[64,512]{0,1:T(8,128)}) %all-reduce.2.cloned.1.call-update) | async-done | bytes 131088 | tf_op jit(solution)/shard_map/psum | solution.py:32
  638.8 1.0 broadcast_multiply_fusion
  639.8 0.8 copy.16
  (8 shorter events, 0.0 us)
Async XLA Ops:
  7.2 218.7 %copy-start = (bf16[512,512]{1,0:T(8,128)(2,1)S(1)}, bf16[512,512]{1,0:T(8,128)(2,1)}, u32[]{:S(2)}) copy-start(bf16[512,512]{1,0:T(8,128)(2,1)} %param.13) | copy-start | bytes 1572868
  7.2 130.4 %all-gather.2.cloned.1.call-start = ((), (), s32[]{:S(2)}) async-start(), calls=%async_computation.2 | async-start | bytes 1064960 | tf_op jit(solution)/shard_map/all_gather | solution.py:15
  8.7 1.3 copy-start.3
  8.7 215.4 %reduce-scatter.4.cloned.1.call-start = ((), (), s32[]{:S(2)}) async-start(), calls=%async_computation.4 | async-start | bytes 1179648
  8.7 1.3 copy-start.2
  137.6 1.6 copy-start.1
  141.2 497.6 %all-reduce.2.cloned.1.call-start = ((), (), s32[]{:S(2)}) async-start(), calls=%async_computation.3 | async-start | bytes 524288 | tf_op jit(solution)/shard_map/psum | solution.py:32
Sparse Core Ops, SparseCore 0:
  10.7 126.8 all-gather.1
  142.0 82.0 reduce-scatter.3
  227.0 411.7 all-reduce.1
where the time goes:
time: 647 us
  waiting for transfers between devices  607 us (94%)
  blocking collectives  15.2 us (2%)
  between operations  13.9 us (2%)
    psum x1, waiting for transfers between devices, body(): grad_weight = lax.psum(part, 'grp')  412 us
    all_gather x1, waiting for transfers between devices, body(): all_masked = lax.all_gather(masked, 'grp', axis=0, tiled=True)  112 us
    unnamed x4, waiting for transfers between devices  82.9 us
    all_to_all x1, blocking collectives, body(): lax.all_to_all(scaled, 'rep', split_axis=1, concat_axis=0, tiled=True)  15.2 us
  transfers between devices with their start and end apart: 3, of which 3 were waited for; matrix products, arithmetic and copies ran while one was open for 0% of the time, Pallas kernels for 0%

commit v1 on v0

--- a/solution.py
+++ b/solution.py
@@ -12,7 +12,9 @@
         jnp.bfloat16
     )
     my_scaled = lax.all_to_all(scaled, "rep", split_axis=1, concat_axis=0, tiled=True)
-    all_masked = lax.all_gather(masked, "grp", axis=0, tiled=True)
+    all_masked = jnp.concatenate(
+        lax.all_to_all(jnp.stack([masked] * lax.axis_size("grp")), "grp", 0, 0), axis=0
+    )
     grad_pre = lax.dot_general(
         my_scaled, all_masked, (((0,), (0,)), ((), ())), preferred_element_type=jnp.float32
     )

time: 647 us -> 600 us (0.927)
  waiting for transfers between devices: 607 us -> 548 us
  starting transfers between devices: 0.12 us -> 25.4 us
  blocking collectives: 15.2 us -> 0 us
    all_gather x1 -> x0, waiting for transfers between devices: 112 us -> none  [body(): all_masked = lax.all_gather(masked, 'grp', axis=0, tiled=True)]
    all_to_all x0 -> x2, waiting for transfers between devices: none -> 61.3 us  [the longest x1 53.7 us: body(): lax.all_to_all(jnp.stack([masked] * lax.axis_size('grp')), 'grp', 0, 0)]
    all_to_all x0 -> x2, starting transfers between devices: none -> 25.3 us  [the longest x1 17.7 us: body(): lax.all_to_all(jnp.stack([masked] * lax.axis_size('grp')), 'grp', 0, 0)]
    all_to_all x1 -> x0, blocking collectives: 15.2 us -> none  [body(): lax.all_to_all(scaled, 'rep', split_axis=1, concat_axis=0, tiled=True)]
    unnamed x4 -> x3, waiting for transfers between devices: 82.9 us -> 76 us
  transfers between devices with their start and end apart: 3 -> 4, of which waited for: 3 -> 4; matrix products, arithmetic and copies ran while one was open for 0% -> 0% of each run, Pallas kernels for 0% -> 0%
where the time goes in v1:
time: 600 us; the launch traced here: 599 us
  waiting for transfers between devices  548 us (91%)
  starting transfers between devices  25.4 us (4%)
  between operations  14.2 us (2%)
  local copies, waits for them, and re-layouts  7.64 us (1%)
    psum x1, waiting for transfers between devices, body(): grad_weight = lax.psum(part, 'grp')  411 us
    unnamed x3, waiting for transfers between devices  76 us
    all_to_all x1, waiting for transfers between devices, body(): lax.all_to_all(jnp.stack([masked] * lax.axis_size('grp')), 'grp', 0, 0)  53.7 us
    all_to_all x1, starting transfers between devices, body(): lax.all_to_all(jnp.stack([masked] * lax.axis_size('grp')), 'grp', 0, 0)  17.7 us
  transfers between devices with their start and end apart: 4, of which 4 were waited for; matrix products, arithmetic and copies ran while one was open for 0% of the time, Pallas kernels for 0%

profile of v1, /device:TPU:1, one launch (start us, length us, event | category | flops | bytes accessed | tf_op | source)
XLA Modules:
  0.0 599.5 jit_solution(16672947544697307248)
XLA Ops:
  7.2 1.3 copy.14
  8.5 0.6 copy-done.5
  9.2 0.9 multiply_convert_fusion
  10.1 7.6 %all-to-all-start = ((bf16[128,8,128]{0,2,1:T(8,128)(2,1)}), bf16[128,8,128]{0,2,1:T(8,128)(2,1)S(1)}, u32[]{:S(2)}, u32[]{:S(2)}) async-start(bf16[128,8,128]{0,2,1:T(8,128)(2,1)} %bitcast), calls=%async_computation | async-start | bytes 524288 | tf_op jit(solution)/shard_map/all_to_all | solution.py:14
  17.7 7.6 %all-to-all-done = bf16[128,8,128]{0,2,1:T(8,128)(2,1)S(1)} async-done(((bf16[128,8,128]{0,2,1:T(8,128)(2,1)}), bf16[128,8,128]{0,2,1:T(8,128)(2,1)S(1)}, u32[]{:S(2)}, u32[]{:S(2)}) %all-to-all-start) | async-done | bytes 262176 | tf_op jit(solution)/shard_map/all_to_all | solution.py:14
  25.4 1.1 stack.2
  26.5 17.7 %all-to-all-start.1 = ((bf16[64,16,512]{2,1,0:T(8,128)(2,1)}), bf16[64,16,512]{2,1,0:T(8,128)(2,1)S(1)}, u32[]{:S(2)}, u32[]{:S(2)}) async-start(bf16[64,16,512]{2,1,0:T(8,128)(2,1)} %stack.2), calls=%async_computation.1 | async-start | bytes 2097152 | tf_op jit(solution)/shard_map/all_to_all | solution.py:16
  44.2 0.0 reduce-scatter.4.cloned.1.call-start
  44.3 0.2 copy.15
  44.4 53.7 %all-to-all-done.1 = bf16[64,16,512]{2,1,0:T(8,128)(2,1)S(1)} async-done(((bf16[64,16,512]{2,1,0:T(8,128)(2,1)}), bf16[64,16,512]{2,1,0:T(8,128)(2,1)S(1)}, u32[]{:S(2)}, u32[]{:S(2)}) %all-to-all-start.1) | async-done | bytes 1048608 | tf_op jit(solution)/shard_map/all_to_all | solution.py:16
  98.1 0.3 fusion.5
  98.4 0.6 copy-done.1
  99.0 0.3 fusion.2
  99.3 0.3 fusion
  99.7 1.3 copy.17
  101.0 0.0 reduce-scatter.4.cloned.1.call-update
  101.0 0.0 all-reduce.2.cloned.1.call-start
  101.1 76.0 %reduce-scatter.4.cloned.1.call-done = f32[64,512]{1,0:T(8,128)} async-done(((f32[512,512]{1,0:T(8,128)}), f32[64,512]{1,0:T(8,128)}) %reduce-scatter.4.cloned.1.call-update) | async-done | bytes 131088
  177.1 1.7 copy.18
  178.8 0.0 all-reduce.2.cloned.1.call-update
  178.8 1.0 convolution_convert_fusion
  179.8 411.1 %all-reduce.2.cloned.1.call-done = f32[64,512]{0,1:T(8,128)} async-done(((f32[64,512]{0,1:T(8,128)}), f32[64,512]{0,1:T(8,128)}) %all-reduce.2.cloned.1.call-update) | async-done | bytes 131088 | tf_op jit(solution)/shard_map/psum | solution.py:34
  590.9 1.0 broadcast_multiply_fusion
  591.9 0.8 copy.16
  (13 shorter events, 0.0 us)
Async XLA Ops:
  7.2 171.7 %copy-start = (bf16[512,512]{1,0:T(8,128)(2,1)S(1)}, bf16[512,512]{1,0:T(8,128)(2,1)}, u32[]{:S(2)}) copy-start(bf16[512,512]{1,0:T(8,128)(2,1)} %param.13) | copy-start | bytes 1572868
  7.2 1.3 copy-start.4
  8.5 0.7 copy-start.5
  10.1 7.6 %copy-start.2 = (s32[16,512]{1,0:T(8,128)S(1)}, s32[16,512]{1,0:T(8,128)}, u32[]{:S(2)}) copy-start(s32[16,512]{1,0:T(8,128)} %param.8) | copy-start | bytes 98308
  10.1 7.6 %copy-start.3 = (bf16[16,512]{1,0:T(8,128)(2,1)S(1)}, bf16[16,512]{1,0:T(8,128)(2,1)}, u32[]{:S(2)}) copy-start(bf16[16,512]{1,0:T(8,128)(2,1)} %param.7) | copy-start | bytes 49156
  10.1 15.3 %all-to-all-start = ((bf16[128,8,128]{0,2,1:T(8,128)(2,1)}), bf16[128,8,128]{0,2,1:T(8,128)(2,1)S(1)}, u32[]{:S(2)}, u32[]{:S(2)}) async-start(bf16[128,8,128]{0,2,1:T(8,128)(2,1)} %bitcast), calls=%async_computation | async-start | bytes 524288 | tf_op jit(solution)/shard_map/all_to_all | solution.py:14
  26.5 71.6 %all-to-all-start.1 = ((bf16[64,16,512]{2,1,0:T(8,128)(2,1)}), bf16[64,16,512]{2,1,0:T(8,128)(2,1)S(1)}, u32[]{:S(2)}, u32[]{:S(2)}) async-start(bf16[64,16,512]{2,1,0:T(8,128)(2,1)} %stack.2), calls=%async_computation.1 | async-start | bytes 2097152 | tf_op jit(solution)/shard_map/all_to_all | solution.py:16
  44.2 132.8 %reduce-scatter.4.cloned.1.call-start = ((), (), s32[]{:S(2)}) async-start(), calls=%async_computation.4 | async-start | bytes 1179648
  98.1 0.9 copy-start.1
  101.0 489.9 %all-reduce.2.cloned.1.call-start = ((), (), s32[]{:S(2)}) async-start(), calls=%async_computation.3 | async-start | bytes 524288 | tf_op jit(solution)/shard_map/psum | solution.py:34
Sparse Core Ops, SparseCore 0:
  101.1 75.8 reduce-scatter.3
  180.0 410.8 all-reduce.1

commit v2 on v0

--- a/solution.py
+++ b/solution.py
@@ -29,7 +29,7 @@
         inputs, low, (((0,), (0,)), ((), ())), preferred_element_type=jnp.float32
     )
     part = lax.psum_scatter(upper + lower, "rep", scatter_dimension=0, tiled=True)
-    grad_weight = lax.psum(part, "grp")
+    grad_weight = jnp.sum(lax.all_gather(part, "grp"), axis=0)
     return (grad_input, grad_weight / vertex_total)
 
 

time: 647 us -> 368 us (0.57)
  waiting for transfers between devices: 607 us -> 323 us
    psum x1 -> x0, waiting for transfers between devices: 412 us -> none  [body(): grad_weight = lax.psum(part, 'grp')]
    all_gather x0 -> x1, waiting for transfers between devices: none -> 131 us  [body(): grad_weight = jnp.sum(lax.all_gather(part, 'grp'), axis=0)]
    unnamed x4 -> x3, waiting for transfers between devices: 82.9 us -> 0.05 us
    reduce_scatter x0 -> x1, waiting for transfers between devices: none -> 82.1 us  [body(): lax.psum_scatter(upper + lower, 'rep', scatter_dimension=0, tiled=True)]
  transfers between devices with their start and end apart: 3 -> 3, of which waited for: 3 -> 3; matrix products, arithmetic and copies ran while one was open for 0% -> 1% of each run, Pallas kernels for 0% -> 0%
where the time goes in v2:
time: 368 us
  waiting for transfers between devices  323 us (88%)
  blocking collectives  15.2 us (4%)
  between operations  13.8 us (4%)
  other arithmetic  7.73 us (2%)
  matrix products  4.96 us (1%)
    all_gather x1, waiting for transfers between devices, body(): grad_weight = jnp.sum(lax.all_gather(part, 'grp'), axis=0)  131 us
    all_gather x1, waiting for transfers between devices, body(): all_masked = lax.all_gather(masked, 'grp', axis=0, tiled=True)  111 us
    reduce_scatter x1, waiting for transfers between devices, body(): lax.psum_scatter(upper + lower, 'rep', scatter_dimension=0, tiled=True)  82.1 us
    all_to_all x1, blocking collectives, body(): lax.all_to_all(scaled, 'rep', split_axis=1, concat_axis=0, tiled=True)  15.2 us
  transfers between devices with their start and end apart: 3, of which 3 were waited for; matrix products, arithmetic and copies ran while one was open for 1% of the time, Pallas kernels for 0%

profile of v2, /device:TPU:1, one launch (start us, length us, event | category | flops | bytes accessed | tf_op | source)
XLA Modules:
  0.0 368.0 jit_solution(275225798145041987)
XLA Ops:
  7.2 0.0 copy-start
  7.2 0.0 all-gather.4.cloned.1.call-start
  7.2 1.4 multiply_convert_fusion.1
  8.6 0.0 all-gather.4.cloned.1.call-update
  8.7 0.0 reduce-scatter.4.cloned.1.call-start
  8.7 1.2 copy.13
  10.0 0.7 convert_rsqrt_fusion.1
  10.6 0.7 convert_rsqrt_fusion
  11.3 0.2 multiply_convert_fusion
  11.5 15.2 %all_to_all.19 = bf16[128,8,128]{0,2,1:T(8,128)(2,1)S(1)} all-to-all(bf16[128,8,128]{0,2,1:T(8,128)(2,1)S(1)} %bitcast.15), channel_id=1, replica_groups=mesh['grp'=64,'rep'=8] {'rep'}, dimensions={1} | all-to-all | bytes 524288 | tf_op jit(solution)/shard_map/all_to_all | solution.py:14
  26.7 0.2 copy.14
  26.9 110.7 %all-gather.4.cloned.1.call-done = bf16[1024,512]{1,0:T(8,128)(2,1)} async-done(((bf16[16,512]{1,0:T(8,128)(2,1)}), bf16[1024,512]{1,0:T(8,128)(2,1)}) %all-gather.4.cloned.1.call-update) | async-done | bytes 1048592 | tf_op jit(solution)/shard_map/all_gather | solution.py:15
  137.6 1.5 fusion.5
  139.1 1.2 fusion.2
  140.4 1.2 fusion
  141.6 1.3 copy.16
  142.9 0.0 reduce-scatter.4.cloned.1.call-update
  142.9 0.0 all-gather.6.cloned.1.call-start
  143.0 82.1 %reduce-scatter.4.cloned.1.call-done = f32[64,512]{1,0:T(8,128)} async-done(((f32[512,512]{1,0:T(8,128)}), f32[64,512]{1,0:T(8,128)}) %reduce-scatter.4.cloned.1.call-update) | async-done | bytes 131088 | tf_op jit(solution)/shard_map/reduce_scatter | solution.py:31
  225.1 0.0 all-gather.6.cloned.1.call-update
  225.1 1.0 convolution_convert_fusion
  226.1 130.6 %all-gather.6.cloned.1.call-done = f32[4096,512]{1,0:T(8,128)} async-done(((f32[64,512]{1,0:T(8,128)}), f32[4096,512]{1,0:T(8,128)}) %all-gather.6.cloned.1.call-update) | async-done | bytes 8388624 | tf_op jit(solution)/shard_map/all_gather | solution.py:32
  356.7 4.1 %reduce_sum.9 = f32[64,512]{1,0:T(8,128)S(1)} reduce(f32[64,64,512]{2,1,0:T(8,128)} %bitcast.12, f32[]{:T(128)} %constant.1.clone.1), dimensions={0}, to_apply=%region_1.0 | reduce | flops 2064384 | bytes 8519684 | tf_op jit(solution)/shard_map/reduce_sum | solution.py:32
  360.8 0.7 broadcast_multiply_fusion
  (1 shorter events, 0.0 us)
Async XLA Ops:
  7.2 218.0 %copy-start = (bf16[512,512]{1,0:T(8,128)(2,1)S(1)}, bf16[512,512]{1,0:T(8,128)(2,1)}, u32[]{:S(2)}) copy-start(bf16[512,512]{1,0:T(8,128)(2,1)} %param.13) | copy-start | bytes 1572868
  7.2 130.4 %all-gather.4.cloned.1.call-start = ((), (), s32[]{:S(2)}) async-start(), calls=%async_computation.2 | async-start | bytes 1064960 | tf_op jit(solution)/shard_map/all_gather | solution.py:15
  8.7 216.4 %reduce-scatter.4.cloned.1.call-start = ((), (), s32[]{:S(2)}) async-start(), calls=%async_computation.4 | async-start | bytes 1179648 | tf_op jit(solution)/shard_map/reduce_scatter | solution.py:31
  142.9 213.8 %all-gather.6.cloned.1.call-start = ((), (), s32[]{:S(2)}) async-start(), calls=%async_computation.3 | async-start | bytes 8519680 | tf_op jit(solution)/shard_map/all_gather | solution.py:32
Sparse Core Ops, SparseCore 0:
  10.7 126.8 all-gather.3
  143.0 82.0 reduce-scatter.3
  227.3 129.4 all-gather.5
